TPU v7x, 256 devices: a whole 4x4x8 slice. The times are simulated.
256 devices in a mesh: sub: 32 (over y_lo, z, core), crow: 4 (over x), ccol: 2 (over y_hi).
Axes of the slice: x: 4, y: 4 (y_hi: 2, y_lo: 2; y = y_hi * 2 + y_lo), z: 8, core: 2. Of those that a mesh axis runs over, the one named last changes fastest.
Arguments:
- rhs: float32 [192, 48, 3, 10, 256], P('sub', ('crow', 'ccol')), may hold values from -6 to 6
- start: float32 [192, 48, 3, 10, 256], P('sub', ('crow', 'ccol')), may hold values from -1.75 to 1.75
- stiffness: float32 [192, 48, 3, 10], P('sub', ('crow', 'ccol')), may hold values from 0.1 to 1
- sub_inverse: bfloat16 [256, 1920, 1920], P(('sub', 'crow', 'ccol')), may hold values from -0.0625 to 0.0625
- basis: bfloat16 [256, 1920, 128], P(('sub', 'crow', 'ccol')), may hold values from -0.0625 to 0.0625
- coarse_inverse: bfloat16 [32, 512, 16384], P(None, ('crow', 'ccol'), 'sub'), may hold values from -0.09375 to 0.09375
- offsets: int32 [32, 8], P('sub'), may hold values from 0 to 464, as said below
Outputs:
- solution: float32 [192, 48, 3, 10, 256], P('sub', ('crow', 'ccol'))
Inputs may be any that keep to these rules, and one draw needn't show every extreme that they name: In every row g, offsets[g, 0] = 0 and the offsets rise; each count (next offset minus this one, 512 after the last) lies between 48 and 128, and every group has a subdomain with exactly 128.
All inputs are finite; a program needn't handle non-finite values.
Results may differ from a plain program's by a relative error of at most 0.0037.
Values may be sent and summed in bfloat16 or wider, within the bound.
A program may use at most 64 MiB of HBM per device.

v0:
```python
import jax
import jax.numpy as jnp
from jax import lax
from jax.sharding import PartitionSpec as P

ITERS = 2


def extended_2(block, sides, width):
    for axis, dim in sides:
        count = lax.axis_size(axis)
        forward = [(i, i + 1) for i in range(count - 1)]
        backward = [(target, source) for source, target in forward]
        low = lax.ppermute(
            lax.slice_in_dim(block, block.shape[dim] - width, None, axis=dim), axis, forward
        )
        high = lax.ppermute(lax.slice_in_dim(block, 0, width, axis=dim), axis, backward)
        block = jnp.concatenate([low, block, high], axis=dim)
    return block


def neighbours(widened):
    padded_z = jnp.pad(widened, ((0, 0), (0, 0), (0, 0), (1, 1), (0, 0)))
    beside = padded_z[2:, 1:-1, :, 1:-1] + padded_z[:-2, 1:-1, :, 1:-1]
    beside = beside + padded_z[1:-1, 2:, :, 1:-1] + padded_z[1:-1, :-2, :, 1:-1]
    beside = beside + padded_z[1:-1, 1:-1, :, 2:] + padded_z[1:-1, 1:-1, :, :-2]
    return beside


def shards(rhs, start, stiffness, sub_inverse, basis, coarse_inverse, offsets):
    cells_s, cells_q, comps, layers, columns = rhs.shape
    kgroup = coarse_inverse.shape[2]
    share_rows = coarse_inverse.shape[1]
    max_cols = basis.shape[2]
    group_offsets = offsets[0]
    groups = group_offsets.shape[0]
    counts = jnp.concatenate([group_offsets[1:], jnp.full((1,), kgroup, jnp.int32)]) - group_offsets
    member = lax.axis_index(("crow", "ccol"))
    sub_index = lax.axis_index("sub")
    member_ids = jnp.arange(groups, dtype=jnp.int32)
    picked = member_ids == member
    own_offset = jnp.sum(jnp.where(picked, group_offsets, 0))
    own_count = jnp.sum(jnp.where(picked, counts, 0))
    col_ids = jnp.arange(max_cols, dtype=jnp.int32)
    wanted = jnp.where(col_ids < own_count, own_offset + col_ids, -1)
    diagonal = (6.0 + stiffness)[..., None]
    flat_inverse = coarse_inverse.reshape(-1, kgroup)
    local_inverse = sub_inverse[0]
    local_basis = basis[0]
    solution = start
    for sweep in range(ITERS):
        widened = extended_2(solution, (("sub", 0), (("crow", "ccol"), 1)), 1)
        residual = rhs - (diagonal * solution - neighbours(widened))
        extended = extended_2(residual.astype(jnp.bfloat16), (("sub", 0), (("crow", "ccol"), 1)), 1)
        flat_res = extended.reshape(-1, columns)
        projected = lax.dot_general(
            local_basis, flat_res, (((0,), (0,)), ((), ())), preferred_element_type=jnp.float32
        )
        restricted = jnp.where(col_ids[:, None] < own_count, projected, 0.0).astype(jnp.bfloat16)
        place_piece = lax.all_gather(restricted, ("crow", "ccol"), axis=0, tiled=True)
        place_row_ids = jnp.arange(place_piece.shape[0], dtype=jnp.int32)
        owner_ids = place_row_ids // max_cols
        column = place_row_ids % max_cols
        matches = member_ids[:, None] == owner_ids[None, :]
        slot_base = jnp.sum(jnp.where(matches, group_offsets[:, None], 0), axis=0)
        slot_limit = jnp.sum(jnp.where(matches, counts[:, None], 0), axis=0)
        targets = jnp.where(column < slot_limit, slot_base + column, -1)
        place_selector = (jnp.arange(kgroup, dtype=jnp.int32)[:, None] == targets[None, :]).astype(
            jnp.bfloat16
        )
        placed_sum = jnp.dot(place_selector, place_piece, preferred_element_type=jnp.float32)
        coefficients = placed_sum.astype(jnp.bfloat16)
        partial_value = jnp.dot(flat_inverse, coefficients, preferred_element_type=jnp.float32)
        summed = lax.psum(partial_value, "sub")
        own_share = lax.dynamic_slice_in_dim(summed, sub_index * share_rows, share_rows, 0)
        amounts = own_share.astype(jnp.bfloat16)
        piece = lax.all_gather(amounts, ("crow", "ccol"), axis=0, tiled=True)
        row_ids = jnp.arange(piece.shape[0], dtype=jnp.int32)
        slot_ids = row_ids % share_rows * groups + row_ids // share_rows
        selector = (wanted[:, None] == slot_ids[None, :]).astype(jnp.bfloat16)
        chosen = jnp.dot(selector, piece, preferred_element_type=jnp.float32)
        chosen = chosen.astype(jnp.bfloat16)
        fine_part = jnp.dot(local_inverse, flat_res, preferred_element_type=jnp.float32)
        coarse_part = jnp.dot(local_basis, chosen, preferred_element_type=jnp.float32)
        correction = (fine_part + coarse_part).reshape(
            cells_s + 2, cells_q + 2, comps, layers, columns
        )
        solution = solution + correction[1:-1, 1:-1]
    return solution


def solution(mesh):
    return jax.shard_map(
        shards,
        mesh=mesh,
        in_specs=(
            P("sub", ("crow", "ccol"), None, None, None),
            P("sub", ("crow", "ccol"), None, None, None),
            P("sub", ("crow", "ccol"), None, None),
            P(("sub", "crow", "ccol"), None, None),
            P(("sub", "crow", "ccol"), None, None),
            P(None, ("crow", "ccol"), "sub"),
            P("sub", None),
        ),
        out_specs=P("sub", ("crow", "ccol"), None, None, None),
        check_vma=False,
    )
```

profile of v0, /device:TPU:32, one launch (start us, length us, event | category | flops | bytes accessed | tf_op | source)
XLA Modules:
  0.0 560.9 jit_solution(5922498140937865681)
XLA Ops:
  5.1 3.6 collective-permute-start
  14.3 6.1 %collective-permute-start.3 = (f32[8,1,3,10,256]{4,3,2,1,0:T(8,128)S(1)}, f32[8,1,3,10,256]{4,3,2,1,0:T(8,128)S(1)}, u32[]{:S(2)}, u32[]{:S(2)}) collective-permute-start(f32[8,1,3,10,256]{4,3,2,1,0:T(8,128)S(1)} %get-tuple-element.11), channel_id=1, source_target_pairs={{0,1},{1,2},{2,3},{3,4},{4,5},{5,6},{6,7},{8,9},{9,10},{10,11},{11... | collective-permute-start | bytes 737288 | tf_op jit(solution)/shard_map/ppermute | solution.py:14
  20.5 6.7 %collective-permute-done.2 = f32[8,1,3,10,256]{4,3,2,1,0:T(8,128)S(1)} collective-permute-done((f32[8,1,3,10,256]{4,3,2,1,0:T(8,128)S(1)}, f32[8,1,3,10,256]{4,3,2,1,0:T(8,128)S(1)}, u32[]{:S(2)}, u32[]{:S(2)}) %collective-permute-start.2) | collective-permute-done | bytes 245792 | tf_op jit(solution)/shard_map/ppermute | solution.py:17
  27.2 9.7 %collective-permute-done.3 = f32[8,1,3,10,256]{4,3,2,1,0:T(8,128)S(1)} collective-permute-done((f32[8,1,3,10,256]{4,3,2,1,0:T(8,128)S(1)}, f32[8,1,3,10,256]{4,3,2,1,0:T(8,128)S(1)}, u32[]{:S(2)}, u32[]{:S(2)}) %collective-permute-start.3) | collective-permute-done | bytes 245792 | tf_op jit(solution)/shard_map/ppermute | solution.py:14
  42.0 3.4 collective-permute-start.5
  48.8 5.9 %collective-permute-start.6 = (bf16[8,1,3,10,256]{4,3,2,1,0:T(8,128)(2,1)}, bf16[8,1,3,10,256]{4,3,2,1,0:T(8,128)(2,1)S(1)}, u32[]{:S(2)}, u32[]{:S(2)}) collective-permute-start(bf16[8,1,3,10,256]{4,3,2,1,0:T(8,128)(2,1)} %get-tuple-element.19), channel_id=1, source_target_pairs={{0,1},{1,2},{2,3},{3,4},{4,5},{5,6},{6,7},{8,9},{9,10},{10,11},{11... | collective-permute-start | bytes 368648 | tf_op jit(solution)/shard_map/ppermute | solution.py:14
  59.1 6.2 %collective-permute-done.7 = bf16[8,1,3,10,256]{4,3,2,1,0:T(8,128)(2,1)} collective-permute-done((bf16[8,1,3,10,256]{4,3,2,1,0:T(8,128)(2,1)}, bf16[8,1,3,10,256]{4,3,2,1,0:T(8,128)(2,1)}, u32[]{:S(2)}, u32[]{:S(2)}) %collective-permute-start.7) | collective-permute-done | bytes 122912 | tf_op jit(solution)/shard_map/ppermute | solution.py:17
  65.3 2.4 pad_maximum_fusion.12
  67.7 3.2 reshape.98
  72.6 31.8 %all_gather.12 = bf16[1024,256]{0,1:T(8,128)(2,1)S(1)} all-gather(bf16[128,256]{0,1:T(8,128)(2,1)S(1)} %fusion.34), channel_id=1, replica_groups=mesh['sub'=32,'crow'=4,'ccol'=2] {'crow','ccol'}, dimensions={0}, use_global_device_ids=true | all-gather | bytes 589824 | tf_op jit(solution)/shard_map/all_gather | solution.py:60
  104.4 2.9 convolution_bitcast_fusion.1
  107.3 122.5 %all-reduce.4 = bf16[2048,256]{1,0:T(8,128)(2,1)} all-reduce(f32[2048,256]{1,0:T(8,128)} %convolution_bitcast_fusion.1), channel_id=1, replica_groups=mesh['sub'=32,'crow'=4,'ccol'=2] {'sub'}, use_global_device_ids=true, to_apply=%region_4.5 | all-reduce | flops 524288 | bytes 3145728 | tf_op jit(solution)/shard_map/psum | solution.py:74
  230.6 34.5 %all_gather.13 = bf16[512,256]{1,0:T(8,128)(2,1)S(1)} all-gather(bf16[64,256]{1,0:T(8,128)(2,1)S(1)} %dynamic-slice_convert_fusion.1), channel_id=1, replica_groups=mesh['sub'=32,'crow'=4,'ccol'=2] {'crow','ccol'}, dimensions={0}, use_global_device_ids=true | all-gather | bytes 294912 | tf_op jit(solution)/shard_map/all_gather | solution.py:77
  267.1 7.6 %fusion.8 = f32[1920,256]{0,1:T(8,128)} fusion(f32[256,1920]{1,0:T(8,128)} %fusion.35, bf16[1920,256]{1,0:T(8,128)(2,1)} %reshape.98, bf16[1,1920,1920]{2,1,0:T(8,128)(2,1)} %param.10), kind=kOutput, calls=%fused_computation.16 | convolution fusion | flops 1887928320 | bytes 12288000 | tf_op jit(solution)/shard_map/dot_general | solution.py:83
  274.6 2.9 copy.59
  277.5 3.4 reshape.100
  289.5 7.1 %collective-permute-done.9 = f32[1,6,3,10,256]{4,3,2,1,0:T(8,128)S(1)} collective-permute-done((f32[1,6,3,10,256]{4,3,2,1,0:T(8,128)S(1)}, f32[1,6,3,10,256]{4,3,2,1,0:T(8,128)S(1)}, u32[]{:S(2)}, u32[]{:S(2)}) %collective-permute-start.9) | collective-permute-done | bytes 184352 | tf_op jit(solution)/shard_map/ppermute | solution.py:14
  298.0 6.2 %collective-permute-start.11 = (f32[8,1,3,10,256]{4,3,2,1,0:T(8,128)S(1)}, f32[8,1,3,10,256]{4,3,2,1,0:T(8,128)S(1)}, u32[]{:S(2)}, u32[]{:S(2)}) collective-permute-start(f32[8,1,3,10,256]{4,3,2,1,0:T(8,128)S(1)} %get-tuple-element.9), channel_id=1, source_target_pairs={{0,1},{1,2},{2,3},{3,4},{4,5},{5,6},{6,7},{8,9},{9,10},{10,11},{11... | collective-permute-start | bytes 737288 | tf_op jit(solution)/shard_map/ppermute | solution.py:14
  304.2 3.6 collective-permute-done.10
  307.8 3.7 collective-permute-done.11
  315.6 8.3 %collective-permute-start.13 = (bf16[1,6,3,10,256]{4,3,2,1,0:T(8,128)(2,1)S(1)}, bf16[1,6,3,10,256]{4,3,2,1,0:T(8,128)(2,1)S(1)}, u32[]{:S(2)}, u32[]{:S(2)}) collective-permute-start(bf16[1,6,3,10,256]{4,3,2,1,0:T(8,128)(2,1)S(1)} %get-tuple-element.22), channel_id=1, source_target_pairs={{8,0},{16,8},{24,16},{32,24},{40,32},{48,40},{56,48},{64,56},{72,6... | collective-permute-start | bytes 276488 | tf_op jit(solution)/shard_map/ppermute | solution.py:17
  326.6 5.7 %collective-permute-start.14 = (bf16[8,1,3,10,256]{4,3,2,1,0:T(8,128)(2,1)S(1)}, bf16[8,1,3,10,256]{4,3,2,1,0:T(8,128)(2,1)S(1)}, u32[]{:S(2)}, u32[]{:S(2)}) collective-permute-start(bf16[8,1,3,10,256]{4,3,2,1,0:T(8,128)(2,1)S(1)} %get-tuple-element.17), channel_id=1, source_target_pairs={{0,1},{1,2},{2,3},{3,4},{4,5},{5,6},{6,7},{8,9},{9,10},{10,11},{11... | collective-permute-start | bytes 368648 | tf_op jit(solution)/shard_map/ppermute | solution.py:14
  335.5 5.9 %collective-permute-done.15 = bf16[8,1,3,10,256]{4,3,2,1,0:T(8,128)(2,1)S(1)} collective-permute-done((bf16[8,1,3,10,256]{4,3,2,1,0:T(8,128)(2,1)S(1)}, bf16[8,1,3,10,256]{4,3,2,1,0:T(8,128)(2,1)S(1)}, u32[]{:S(2)}, u32[]{:S(2)}) %collective-permute-start.15) | collective-permute-done | bytes 122912 | tf_op jit(solution)/shard_map/ppermute | solution.py:17
  342.9 3.2 reshape.101
  347.7 30.9 %all_gather.14 = bf16[1024,256]{0,1:T(8,128)(2,1)S(1)} all-gather(bf16[128,256]{0,1:T(8,128)(2,1)S(1)} %fusion.33), channel_id=1, replica_groups=mesh['sub'=32,'crow'=4,'ccol'=2] {'crow','ccol'}, dimensions={0}, use_global_device_ids=true | all-gather | bytes 589824 | tf_op jit(solution)/shard_map/all_gather | solution.py:60
  378.7 2.9 convolution_bitcast_fusion
  381.6 123.6 %all-reduce.5 = bf16[2048,256]{1,0:T(8,128)(2,1)} all-reduce(f32[2048,256]{1,0:T(8,128)} %convolution_bitcast_fusion), channel_id=1, replica_groups=mesh['sub'=32,'crow'=4,'ccol'=2] {'sub'}, use_global_device_ids=true, to_apply=%region_5.6 | all-reduce | flops 524288 | bytes 3145728 | tf_op jit(solution)/shard_map/psum | solution.py:74
  506.0 34.6 %all_gather.15 = bf16[512,256]{1,0:T(8,128)(2,1)S(1)} all-gather(bf16[64,256]{1,0:T(8,128)(2,1)S(1)} %dynamic-slice_convert_fusion), channel_id=1, replica_groups=mesh['sub'=32,'crow'=4,'ccol'=2] {'crow','ccol'}, dimensions={0}, use_global_device_ids=true | all-gather | bytes 294912 | tf_op jit(solution)/shard_map/all_gather | solution.py:77
  542.6 7.6 %fusion.14 = f32[1920,256]{0,1:T(8,128)} fusion(f32[256,1920]{1,0:T(8,128)} %fusion.36, bf16[1920,256]{1,0:T(8,128)(2,1)} %reshape.101, bf16[1,1920,1920]{2,1,0:T(8,128)(2,1)} %param.10), kind=kOutput, calls=%fused_computation.18 | convolution fusion | flops 1887928320 | bytes 12288000 | tf_op jit(solution)/shard_map/dot_general | solution.py:83
  550.2 2.9 copy.63
  553.0 3.4 reshape.102
  556.4 2.4 slice_add_fusion
  (76 shorter events, 55.7 us)
Async XLA Ops:
  0.0 104.4 %copy-start = (bf16[32,64,512]{2,1,0:T(8,128)(2,1)S(1)}, bf16[32,64,512]{2,1,0:T(8,128)(2,1)}, u32[]{:S(2)}) copy-start(bf16[32,64,512]{2,1,0:T(8,128)(2,1)} %param.12) | copy-start | bytes 6291460
  0.0 8.7 %copy-start.11 = (s32[1,8]{1,0:T(1,128)S(1)}, s32[1,8]{1,0:T(1,128)}, u32[]{:S(2)}) copy-start(s32[1,8]{1,0:T(1,128)} %param.13) | copy-start | bytes 100
  1.8 1.2 copy-start.2
  3.1 8.0 %collective-permute-start.1 = (f32[1,6,3,10,256]{4,3,2,1,0:T(8,128)S(1)}, f32[1,6,3,10,256]{4,3,2,1,0:T(8,128)S(1)}, u32[]{:S(2)}, u32[]{:S(2)}) collective-permute-start(f32[1,6,3,10,256]{4,3,2,1,0:T(8,128)S(1)} %get-tuple-element.16), channel_id=1, source_target_pairs={{0,8},{8,16},{16,24},{24,32},{32,40},{40,48},{48,56},{56,64},{64,7... | collective-permute-start | bytes 552968 | tf_op jit(solution)/shard_map/ppermute | solution.py:14
  5.1 7.9 %collective-permute-start = (f32[1,6,3,10,256]{4,3,2,1,0:T(8,128)S(1)}, f32[1,6,3,10,256]{4,3,2,1,0:T(8,128)S(1)}, u32[]{:S(2)}, u32[]{:S(2)}) collective-permute-start(f32[1,6,3,10,256]{4,3,2,1,0:T(8,128)S(1)} %get-tuple-element.15), channel_id=1, source_target_pairs={{8,0},{16,8},{24,16},{32,24},{40,32},{48,40},{56,48},{64,56},{72,6... | collective-permute-start | bytes 552968 | tf_op jit(solution)/shard_map/ppermute | solution.py:17
  12.9 7.5 %copy-start.8 = (f32[6,6,3,10]{3,2,1,0:T(4,128)S(1)}, f32[6,6,3,10]{3,2,1,0:T(4,128)}, u32[]{:S(2)}) copy-start(f32[6,6,3,10]{3,2,1,0:T(4,128)} %param.9) | copy-start | bytes 12964
  12.9 23.9 %copy-start.7 = (f32[1,6,3,10,256]{4,3,2,1,0:T(8,128)}, f32[1,6,3,10,256]{4,3,2,1,0:T(8,128)S(1)}, u32[]{:S(2)}) copy-start(f32[1,6,3,10,256]{4,3,2,1,0:T(8,128)S(1)} %collective-permute-done) | copy-start | bytes 552964
  13.0 14.2 %collective-permute-start.2 = (f32[8,1,3,10,256]{4,3,2,1,0:T(8,128)S(1)}, f32[8,1,3,10,256]{4,3,2,1,0:T(8,128)S(1)}, u32[]{:S(2)}, u32[]{:S(2)}) collective-permute-start(f32[8,1,3,10,256]{4,3,2,1,0:T(8,128)S(1)} %get-tuple-element.12), channel_id=1, source_target_pairs={{1,0},{2,1},{3,2},{4,3},{5,4},{6,5},{7,6},{9,8},{10,9},{11,10},{12... | collective-permute-start | bytes 737288 | tf_op jit(solution)/shard_map/ppermute | solution.py:17
  14.3 22.5 %collective-permute-start.3 = (f32[8,1,3,10,256]{4,3,2,1,0:T(8,128)S(1)}, f32[8,1,3,10,256]{4,3,2,1,0:T(8,128)S(1)}, u32[]{:S(2)}, u32[]{:S(2)}) collective-permute-start(f32[8,1,3,10,256]{4,3,2,1,0:T(8,128)S(1)} %get-tuple-element.11), channel_id=1, source_target_pairs={{0,1},{1,2},{2,3},{3,4},{4,5},{5,6},{6,7},{8,9},{9,10},{10,11},{11... | collective-permute-start | bytes 737288 | tf_op jit(solution)/shard_map/ppermute | solution.py:14
  20.4 17.0 %copy-start.3 = (f32[6,6,3,10,256]{4,3,2,1,0:T(8,128)S(1)}, f32[6,6,3,10,256]{4,3,2,1,0:T(8,128)}, u32[]{:S(2)}) copy-start(f32[6,6,3,10,256]{4,3,2,1,0:T(8,128)} %copy-done.2) | copy-start | bytes 3317764
  20.5 17.0 %copy-start.5 = (f32[6,6,3,10,256]{4,2,3,1,0:T(4,128)S(1)}, f32[6,6,3,10,256]{4,2,3,1,0:T(4,128)}, u32[]{:S(2)}) copy-start(f32[6,6,3,10,256]{4,2,3,1,0:T(4,128)} %param.7) | copy-start | bytes 3317764
  39.8 6.7 %collective-permute-start.4 = (bf16[1,6,3,10,256]{4,3,2,1,0:T(8,128)(2,1)S(1)}, bf16[1,6,3,10,256]{4,3,2,1,0:T(8,128)(2,1)S(1)}, u32[]{:S(2)}, u32[]{:S(2)}) collective-permute-start(bf16[1,6,3,10,256]{4,3,2,1,0:T(8,128)(2,1)S(1)} %get-tuple-element.23), channel_id=1, source_target_pairs={{0,8},{8,16},{16,24},{24,32},{32,40},{40,48},{48,56},{56,64},{64,7... | collective-permute-start | bytes 276488 | tf_op jit(solution)/shard_map/ppermute | solution.py:14
  42.0 6.0 %collective-permute-start.5 = (bf16[1,6,3,10,256]{4,3,2,1,0:T(8,128)(2,1)S(1)}, bf16[1,6,3,10,256]{4,3,2,1,0:T(8,128)(2,1)S(1)}, u32[]{:S(2)}, u32[]{:S(2)}) collective-permute-start(bf16[1,6,3,10,256]{4,3,2,1,0:T(8,128)(2,1)S(1)} %get-tuple-element.24), channel_id=1, source_target_pairs={{8,0},{16,8},{24,16},{32,24},{40,32},{48,40},{56,48},{64,56},{72,6... | collective-permute-start | bytes 276488 | tf_op jit(solution)/shard_map/ppermute | solution.py:17
  48.8 10.3 %collective-permute-start.6 = (bf16[8,1,3,10,256]{4,3,2,1,0:T(8,128)(2,1)}, bf16[8,1,3,10,256]{4,3,2,1,0:T(8,128)(2,1)S(1)}, u32[]{:S(2)}, u32[]{:S(2)}) collective-permute-start(bf16[8,1,3,10,256]{4,3,2,1,0:T(8,128)(2,1)} %get-tuple-element.19), channel_id=1, source_target_pairs={{0,1},{1,2},{2,3},{3,4},{4,5},{5,6},{6,7},{8,9},{9,10},{10,11},{11... | collective-permute-start | bytes 368648 | tf_op jit(solution)/shard_map/ppermute | solution.py:14
  54.7 10.6 %collective-permute-start.7 = (bf16[8,1,3,10,256]{4,3,2,1,0:T(8,128)(2,1)}, bf16[8,1,3,10,256]{4,3,2,1,0:T(8,128)(2,1)}, u32[]{:S(2)}, u32[]{:S(2)}) collective-permute-start(bf16[8,1,3,10,256]{4,3,2,1,0:T(8,128)(2,1)} %get-tuple-element.20), channel_id=1, source_target_pairs={{1,0},{2,1},{3,2},{4,3},{5,4},{6,5},{7,6},{9,8},{10,9},{11,10},{12... | collective-permute-start | bytes 368648 | tf_op jit(solution)/shard_map/ppermute | solution.py:17
  67.7 3.2 copy-start.4
  67.7 3.2 copy-start.9
  107.3 157.7 %copy-start.10 = (s32[128]{0:T(128)S(1)}, s32[128]{0:T(128)}, u32[]{:S(2)}) copy-start(s32[128]{0:T(128)} %add_select_fusion.4) | copy-start | bytes 1540
  283.3 29.0 %copy-start.1 = (f32[6,6,3,10,256]{4,3,2,1,0:T(8,128)}, f32[6,6,3,10,256]{4,3,2,1,0:T(8,128)S(1)}, u32[]{:S(2)}) copy-start(f32[6,6,3,10,256]{4,3,2,1,0:T(8,128)S(1)} %slice_add_fusion.3) | copy-start | bytes 3317764
  283.3 6.1 %collective-permute-start.8 = (f32[1,6,3,10,256]{4,3,2,1,0:T(8,128)S(1)}, f32[1,6,3,10,256]{4,3,2,1,0:T(8,128)S(1)}, u32[]{:S(2)}, u32[]{:S(2)}) collective-permute-start(f32[1,6,3,10,256]{4,3,2,1,0:T(8,128)S(1)} %get-tuple-element.14), channel_id=1, source_target_pairs={{8,0},{16,8},{24,16},{32,24},{40,32},{48,40},{56,48},{64,56},{72,6... | collective-permute-start | bytes 552968 | tf_op jit(solution)/shard_map/ppermute | solution.py:17
  285.2 11.3 %collective-permute-start.9 = (f32[1,6,3,10,256]{4,3,2,1,0:T(8,128)S(1)}, f32[1,6,3,10,256]{4,3,2,1,0:T(8,128)S(1)}, u32[]{:S(2)}, u32[]{:S(2)}) collective-permute-start(f32[1,6,3,10,256]{4,3,2,1,0:T(8,128)S(1)} %get-tuple-element.13), channel_id=1, source_target_pairs={{0,8},{8,16},{16,24},{24,32},{32,40},{40,48},{48,56},{56,64},{64,7... | collective-permute-start | bytes 552968 | tf_op jit(solution)/shard_map/ppermute | solution.py:14
  296.7 11.2 %collective-permute-start.10 = (f32[8,1,3,10,256]{4,3,2,1,0:T(8,128)S(1)}, f32[8,1,3,10,256]{4,3,2,1,0:T(8,128)S(1)}, u32[]{:S(2)}, u32[]{:S(2)}) collective-permute-start(f32[8,1,3,10,256]{4,3,2,1,0:T(8,128)S(1)} %get-tuple-element.10), channel_id=1, source_target_pairs={{1,0},{2,1},{3,2},{4,3},{5,4},{6,5},{7,6},{9,8},{10,9},{11,10},{12... | collective-permute-start | bytes 737288 | tf_op jit(solution)/shard_map/ppermute | solution.py:17
  298.0 14.3 %copy-start.6 = (f32[6,6,3,10,256]{4,2,3,1,0:T(4,128)S(1)}, f32[6,6,3,10,256]{4,2,3,1,0:T(4,128)}, u32[]{:S(2)}) copy-start(f32[6,6,3,10,256]{4,2,3,1,0:T(4,128)} %param.7) | copy-start | bytes 3317764
  298.0 13.6 %collective-permute-start.11 = (f32[8,1,3,10,256]{4,3,2,1,0:T(8,128)S(1)}, f32[8,1,3,10,256]{4,3,2,1,0:T(8,128)S(1)}, u32[]{:S(2)}, u32[]{:S(2)}) collective-permute-start(f32[8,1,3,10,256]{4,3,2,1,0:T(8,128)S(1)} %get-tuple-element.9), channel_id=1, source_target_pairs={{0,1},{1,2},{2,3},{3,4},{4,5},{5,6},{6,7},{8,9},{9,10},{10,11},{11... | collective-permute-start | bytes 737288 | tf_op jit(solution)/shard_map/ppermute | solution.py:14
  313.6 11.1 %collective-permute-start.12 = (bf16[1,6,3,10,256]{4,3,2,1,0:T(8,128)(2,1)S(1)}, bf16[1,6,3,10,256]{4,3,2,1,0:T(8,128)(2,1)S(1)}, u32[]{:S(2)}, u32[]{:S(2)}) collective-permute-start(bf16[1,6,3,10,256]{4,3,2,1,0:T(8,128)(2,1)S(1)} %get-tuple-element.21), channel_id=1, source_target_pairs={{0,8},{8,16},{16,24},{24,32},{32,40},{40,48},{48,56},{56,64},{64,7... | collective-permute-start | bytes 276488 | tf_op jit(solution)/shard_map/ppermute | solution.py:14
  315.6 11.0 %collective-permute-start.13 = (bf16[1,6,3,10,256]{4,3,2,1,0:T(8,128)(2,1)S(1)}, bf16[1,6,3,10,256]{4,3,2,1,0:T(8,128)(2,1)S(1)}, u32[]{:S(2)}, u32[]{:S(2)}) collective-permute-start(bf16[1,6,3,10,256]{4,3,2,1,0:T(8,128)(2,1)S(1)} %get-tuple-element.22), channel_id=1, source_target_pairs={{8,0},{16,8},{24,16},{32,24},{40,32},{48,40},{56,48},{64,56},{72,6... | collective-permute-start | bytes 276488 | tf_op jit(solution)/shard_map/ppermute | solution.py:17
  326.6 8.9 %collective-permute-start.14 = (bf16[8,1,3,10,256]{4,3,2,1,0:T(8,128)(2,1)S(1)}, bf16[8,1,3,10,256]{4,3,2,1,0:T(8,128)(2,1)S(1)}, u32[]{:S(2)}, u32[]{:S(2)}) collective-permute-start(bf16[8,1,3,10,256]{4,3,2,1,0:T(8,128)(2,1)S(1)} %get-tuple-element.17), channel_id=1, source_target_pairs={{0,1},{1,2},{2,3},{3,4},{4,5},{5,6},{6,7},{8,9},{9,10},{10,11},{11... | collective-permute-start | bytes 368648 | tf_op jit(solution)/shard_map/ppermute | solution.py:14
  332.3 9.1 %collective-permute-start.15 = (bf16[8,1,3,10,256]{4,3,2,1,0:T(8,128)(2,1)S(1)}, bf16[8,1,3,10,256]{4,3,2,1,0:T(8,128)(2,1)S(1)}, u32[]{:S(2)}, u32[]{:S(2)}) collective-permute-start(bf16[8,1,3,10,256]{4,3,2,1,0:T(8,128)(2,1)S(1)} %get-tuple-element.18), channel_id=1, source_target_pairs={{1,0},{2,1},{3,2},{4,3},{5,4},{6,5},{7,6},{9,8},{10,9},{11,10},{12... | collective-permute-start | bytes 368648 | tf_op jit(solution)/shard_map/ppermute | solution.py:17
where the time goes:
time: 571 us; the launch traced here: 561 us
  blocking collectives  378 us (66%)
  starting transfers between devices  54.7 us (10%)
  waiting for transfers between devices  53.7 us (9%)
  matrix products  28.4 us (5%)
  local copies, waits for them, and re-layouts  27.4 us (5%)
  other arithmetic  18.3 us (3%)
    psum x2, blocking collectives, shards(): summed = lax.psum(partial_value, 'sub')  246 us
    all_gather x2, blocking collectives, shards(): piece = lax.all_gather(amounts, ('crow', 'ccol'), axis=0, tiled=True)  69.1 us
    all_gather x2, blocking collectives, shards(): lax.all_gather(restricted, ('crow', 'ccol'), axis=0, tiled=True)  62.7 us
    ppermute x8, starting transfers between devices, extended_2(): lax.ppermute(lax.slice_in_dim(block, block.shape[dim] - width, None, axis...  32.3 us
    ppermute x8, waiting for transfers between devices, extended_2(): lax.ppermute(lax.slice_in_dim(block, 0, width, axis=dim), axis, backward)  27.6 us
    ppermute x8, waiting for transfers between devices, extended_2(): lax.ppermute(lax.slice_in_dim(block, block.shape[dim] - width, None, axis...  26.1 us
    ppermute x8, starting transfers between devices, extended_2(): lax.ppermute(lax.slice_in_dim(block, 0, width, axis=dim), axis, backward)  22.4 us
    dot_general x2, matrix products, shards(): jnp.dot(local_inverse, flat_res, preferred_element_type=jnp.float32)  15.2 us
  transfers between devices with their start and end apart: 16, of which 14 were waited for; matrix products, arithmetic and copies ran while one was open for 1% of the time, Pallas kernels for 0%

commit v1 on v0

v1 whole, which is shorter than its diff:
```python
import functools

import jax
import jax.numpy as jnp
from jax import lax
from jax.experimental import pallas as pl
from jax.experimental.pallas import tpu as pltpu
from jax.sharding import PartitionSpec as P

MESH = pl.DeviceIdType.MESH
SWEEPS = 2
SIDE = 6
EXT = 8
ROWS = 30
CELL = 32
SLAB = EXT * ROWS
PADSLAB = EXT * CELL
INNER = SIDE * CELL
NLOC = EXT * SLAB
LANES = 256
MEMBERS = 8
KMAX = 128
KGROUP = 512
SHARE = 64
NZ = 8
ZORDER = (4, 3, 5, 2, 6, 1, 7, 0)
F32 = jnp.float32
BF16 = jnp.bfloat16


def iota(shape, dim):
    return lax.broadcasted_iota(jnp.int32, shape, dim)


def one_hot(mask):
    return jnp.where(mask, 1.0, 0.0).astype(BF16)


def dot(a, b):
    return jnp.dot(a, b, preferred_element_type=F32)


def kernel(
    nch,
    offs,
    start_hbm,
    rhs,
    diag,
    w_hbm,
    basis_hbm,
    c_hbm,
    out,
    uext,
    res,
    loc,
    locc,
    wraw,
    wp,
    braw,
    bint,
    bt,
    cbuf,
    place,
    pick,
    fine,
    pb,
    hsend,
    hrecv,
    csend_corner,
    crecv_corner,
    pieces,
    cores,
    corer,
    ysend,
    yrecv,
    zsend,
    zrecv,
    cvals,
    load_sem,
    halo_s,
    halo_r,
    g1_s,
    g1_r,
    core_s,
    core_r,
    y_s,
    y_r,
    z_s,
    z_r,
    g2_s,
    g2_r,
):
    width = LANES // nch
    g = lax.axis_index("sub")
    crow = lax.axis_index("crow")
    ccol = lax.axis_index("ccol")
    m = crow * 2 + ccol
    core = lax.rem(g, 2)
    z = lax.rem(g // 2, NZ)
    ylo = g // (2 * NZ)

    def at(gg, mm):
        return (gg, mm // 2, lax.rem(mm, 2))

    def sub_of(yy, zz, cc):
        return (yy * NZ + zz) * 2 + cc

    gp, gm = lax.rem(g + 1, 32), lax.rem(g + 31, 32)
    mp, mm = lax.rem(m + 1, MEMBERS), lax.rem(m + 7, MEMBERS)
    halo_to = [
        at(gp, m), at(gm, m), at(g, mp), at(g, mm),
        at(gp, mp), at(gp, mm), at(gm, mp), at(gm, mm),
    ]
    group_to = [at(g, lax.rem(m + j, MEMBERS)) for j in range(MEMBERS)]
    core_to = at(sub_of(ylo, z, 1 - core), m)
    y_to = at(sub_of(1 - ylo, z, core), m)
    z_to = [at(sub_of(ylo, lax.rem(z + k, NZ), core), m) for k in range(NZ)]
    partners = halo_to + group_to[1:] + [core_to, y_to] + z_to[1:]

    barrier = pltpu.get_barrier_semaphore()
    for device in partners:
        pl.semaphore_signal(barrier, inc=1, device_id=device, device_id_type=MESH)

    loads = [
        pltpu.make_async_copy(
            start_hbm, uext.at[pl.ds(1, SIDE), pl.ds(1, SIDE)], load_sem.at[0]
        ),
        pltpu.make_async_copy(basis_hbm, braw, load_sem.at[1]),
        pltpu.make_async_copy(c_hbm.at[:, 0], cbuf.at[0], load_sem.at[2]),
        pltpu.make_async_copy(c_hbm.at[:, 1], cbuf.at[1], load_sem.at[3]),
    ] + [
        pltpu.make_async_copy(
            w_hbm.at[pl.ds((s + 1) * SLAB + 24, INNER)], wraw.at[s], load_sem.at[4 + s]
        )
        for s in range(SIDE)
    ]
    for copy in loads:
        copy.start()

    zero_row = jnp.zeros((EXT, CELL, LANES), F32)
    uext[0] = zero_row
    uext[EXT - 1] = zero_row
    for s in range(1, EXT - 1):
        uext[s, 0] = zero_row[0]
        uext[s, EXT - 1] = zero_row[0]

    row = iota((CELL, 128), 0)
    layer = lax.rem(row, 10)
    has_below = layer != 0
    has_above = jnp.logical_and(layer != 9, row < ROWS)
    ok_sm, ok_sp, ok_qm, ok_qp = g > 0, g < 31, m > 0, m < MEMBERS - 1

    def remote(src, dst, send, recv, device):
        return pltpu.make_async_remote_copy(
            src_ref=src,
            dst_ref=dst,
            send_sem=send,
            recv_sem=recv,
            device_id=device,
            device_id_type=MESH,
        )

    def halo_copies(t, c):
        out_copies = []
        for d in range(4):
            out_copies.append(
                remote(
                    hsend.at[t, c, d], hrecv.at[t, c, d],
                    halo_s.at[t, c, d], halo_r.at[t, c, d], halo_to[d],
                )
            )
        for d in range(4):
            out_copies.append(
                remote(
                    csend_corner.at[t, c, d], crecv_corner.at[t, c, d],
                    halo_s.at[t, c, 4 + d], halo_r.at[t, c, 4 + d], halo_to[4 + d],
                )
            )
        return out_copies

    def lane_tiles(c):
        return [(c * width + i * 128, i * 128) for i in range(width // 128)]

    def stencil(t, c):
        base = rhs if t == 0 else res

        def step(s, carry):
            for lane, _ in lane_tiles(c):
                ls = pl.ds(lane, 128)
                for q in range(SIDE):
                    u = uext[s + 1, q + 1, :, ls]
                    beside = (
                        uext[s, q + 1, :, ls] + uext[s + 2, q + 1, :, ls]
                        + uext[s + 1, q, :, ls] + uext[s + 1, q + 2, :, ls]
                    )
                    beside = beside + jnp.where(has_below, pltpu.roll(u, 1, 0), 0.0)
                    beside = beside + jnp.where(has_above, pltpu.roll(u, CELL - 1, 0), 0.0)
                    res[s, q, :, ls] = base[s, q, :, ls] - (diag[s, q] * u - beside)
            return carry

        lax.fori_loop(0, SIDE, step, 0)
        for lane, dst in lane_tiles(c):
            ls, ds = pl.ds(lane, 128), pl.ds(dst, 128)
            for i in range(SIDE):
                for d, (s, q) in enumerate(((SIDE - 1, i), (0, i), (i, SIDE - 1), (i, 0))):
                    hsend[t, c, d, 0, i, :, ds] = uext[s + 1, q + 1, :, ls].astype(BF16)
                    hsend[t, c, d, 1, i, :, ds] = res[s, q, :, ls].astype(BF16)
            for d, (s, q) in enumerate(((5, 5), (5, 0), (0, 5), (0, 0))):
                csend_corner[t, c, d, 0, :, ds] = uext[s + 1, q + 1, :, ls].astype(BF16)
                csend_corner[t, c, d, 1, :, ds] = res[s, q, :, ls].astype(BF16)

    def finish_residual(t, c):
        for lane, dst in lane_tiles(c):
            ls, ds = pl.ds(lane, 128), pl.ds(dst, 128)

            def got(d, field, i, ok):
                return jnp.where(ok, hrecv[t, c, d, field, i, :, ds].astype(F32), 0.0)

            def corner(d, field, ok):
                return jnp.where(ok, crecv_corner[t, c, d, field, :, ds].astype(F32), 0.0)

            oks = (ok_sm, ok_sp, ok_qm, ok_qp)
            diag_ok = (
                jnp.logical_and(ok_sm, ok_qm), jnp.logical_and(ok_sm, ok_qp),
                jnp.logical_and(ok_sp, ok_qm), jnp.logical_and(ok_sp, ok_qp),
            )
            cu = [corner(d, 0, diag_ok[d]) for d in range(4)]
            for s in range(SIDE):
                for q in range(SIDE):
                    value = res[s, q, :, ls]
                    edge = False
                    for d, here, i in ((0, s == 0, q), (1, s == 5, q), (2, q == 0, s), (3, q == 5, s)):
                        if here:
                            value = value + got(d, 0, i, oks[d])
                            edge = True
                    if edge:
                        res[s, q, :, ls] = value
                    loc[s + 1, q + 1, :, ls] = value.astype(BF16)
            for d in range(4):
                for i in range(SIDE):
                    s, q = ((0, i), (5, i), (i, 0), (i, 5))[d]
                    value = hrecv[t, c, d, 1, i, :, ds].astype(F32) + uext[s + 1, q + 1, :, ls]
                    if i == 0:
                        value = value + cu[(0, 2, 0, 1)[d]]
                    if i == SIDE - 1:
                        value = value + cu[(1, 3, 2, 3)[d]]
                    value = jnp.where(oks[d], value, 0.0).astype(BF16)
                    s, q = ((0, i + 1), (7, i + 1), (i + 1, 0), (i + 1, 7))[d]
                    loc[s, q, :, ls] = value
            for d in range(4):
                sd, qd = ((0, 2), (0, 3), (1, 2), (1, 3))[d]
                si, qi = ((0, 0), (5, 0), (0, 5), (5, 5))[d]
                value = crecv_corner[t, c, d, 1, :, ds].astype(F32)
                value = value + hrecv[t, c, sd, 0, si, :, ds].astype(F32)
                value = value + hrecv[t, c, qd, 0, qi, :, ds].astype(F32)
                value = jnp.where(diag_ok[d], value, 0.0).astype(BF16)
                s, q = ((0, 0), (0, 7), (7, 0), (7, 7))[d]
                loc[s, q, :, ls] = value

    own_offset = offs[m]
    own_count = jnp.where(m == MEMBERS - 1, KGROUP, offs[jnp.minimum(m + 1, MEMBERS - 1)]) - own_offset

    def tables():
        slot = iota((KGROUP, KMAX), 0)
        k = iota((KGROUP, KMAX), 1)
        for j in range(MEMBERS):
            first = offs[j]
            limit = (KGROUP if j == MEMBERS - 1 else offs[j + 1]) - first
            place[:, j * KMAX:(j + 1) * KMAX] = one_hot(
                jnp.logical_and(slot == first + k, k < limit)
            )
        k = iota((KMAX, KGROUP), 0)
        index = iota((KMAX, KGROUP), 1)
        slot = (index % SHARE) * MEMBERS + index // SHARE
        pick[...] = one_hot(jnp.logical_and(slot == own_offset + k, k < own_count))

    def expand_basis():
        j, i = iota((PADSLAB, SLAB), 0), iota((PADSLAB, SLAB), 1)
        spread = one_hot(
            jnp.logical_and(i == (j // CELL) * ROWS + j % CELL, j % CELL < ROWS)
        )
        for s in range(EXT):
            part = dot(spread, braw[s * SLAB:(s + 1) * SLAB, :])
            bt[:, s * PADSLAB:(s + 1) * PADSLAB] = part.T.astype(BF16)
            if 1 <= s <= SIDE:
                bint[(s - 1) * INNER:s * INNER, :] = part[CELL:CELL + INNER, :].astype(BF16)

    def expand_inverse():
        j, i = iota((INNER, INNER), 0), iota((INNER, INNER), 1)
        spread = one_hot(
            jnp.logical_and(i == 6 + (j // CELL) * ROWS + j % CELL, j % CELL < ROWS)
        )

        def step(s, carry):
            wp[pl.ds(pl.multiple_of(s * INNER, INNER), INNER), :] = dot(
                spread, wraw[s]
            ).astype(BF16)
            return carry

        lax.fori_loop(0, SIDE, step, 0)

    def gather_one(t, c):
        return [
            remote(
                pieces.at[t, c, m], pieces.at[t, c, m],
                g1_s.at[t, c, j], g1_r.at[t, c, j], group_to[j],
            )
            for j in range(1, MEMBERS)
        ]

    def gather_two(t, c):
        return [
            remote(
                cvals.at[t, c, m], cvals.at[t, c, m],
                g2_s.at[t, c, j], g2_r.at[t, c, j], group_to[j],
            )
            for j in range(1, MEMBERS)
        ]

    def restrict(t, c):
        ls = pl.ds(c * width, width)
        local = loc[:, :, :, ls].reshape(EXT * PADSLAB, width)
        projected = dot(bt[...], local)
        keep = iota((KMAX, width), 0) < own_count
        pieces[t, c, m] = jnp.where(keep, projected, 0.0).astype(BF16)

    def fine_product(c):
        ls = pl.ds(c * width, width)
        i, j = iota((SLAB, PADSLAB), 0), iota((SLAB, PADSLAB), 1)
        pack = one_hot(
            jnp.logical_and(i == (j // CELL) * ROWS + j % CELL, j % CELL < ROWS)
        )
        for s in range(EXT):
            locc[s * SLAB:(s + 1) * SLAB, ls] = dot(
                pack, loc[s, :, :, ls].reshape(PADSLAB, width)
            ).astype(BF16)
        fine[:, ls] = dot(wp[...], locc[:, ls])

    def core_copies(t, c):
        return [
            remote(
                cores.at[t, c, h], corer.at[t, c, h],
                core_s.at[t, c, h], core_r.at[t, c, h], core_to,
            )
            for h in range(2)
        ]

    def y_copies(t, c):
        return [
            remote(
                ysend.at[t, c, k], yrecv.at[t, c, k],
                y_s.at[t, c, k], y_r.at[t, c, k], y_to,
            )
            for k in range(NZ)
        ]

    def z_copies(t, c):
        return [
            remote(
                zsend.at[t, c, k], zrecv.at[t, c, k],
                z_s.at[t, c, k], z_r.at[t, c, k], z_to[k],
            )
            for k in range(NZ)
        ]

    def coarse(t, c):
        coef = dot(place[...], pieces[t, c].reshape(MEMBERS * KMAX, width)).astype(BF16)
        copies = core_copies(t, c)
        for h, half in ((0, 1 - ylo), (1, ylo)):
            rows = cbuf[1 - core, pl.ds(half * NZ, NZ)].reshape(NZ * SHARE, KGROUP)
            cores[t, c, h] = dot(rows, coef).astype(BF16).reshape(NZ, SHARE, width)
            copies[h].start()
        for h, half in ((0, 1 - ylo), (1, ylo)):
            rows = cbuf[core, pl.ds(half * NZ, NZ)].reshape(NZ * SHARE, KGROUP)
            pb[c, h] = dot(rows, coef).reshape(NZ, SHARE, width)

    def reduce_sums(t, c):
        copies, ys, zs = core_copies(t, c), y_copies(t, c), z_copies(t, c)
        copies[0].wait_recv()
        for k in ZORDER:
            zz = lax.rem(z + k, NZ)
            ysend[t, c, k] = (pb[c, 0, zz] + corer[t, c, 0, zz].astype(F32)).astype(BF16)
            ys[k].start()
        copies[1].wait_recv()
        for k in ZORDER:
            zz = lax.rem(z + k, NZ)
            ys[k].wait_recv()
            value = pb[c, 1, zz] + corer[t, c, 1, zz].astype(F32) + yrecv[t, c, k].astype(F32)
            if k == 0:
                total = value
            else:
                zsend[t, c, k] = value.astype(BF16)
                zs[k].start()
        for k in ZORDER[::-1]:
            if k:
                zs[k].wait_recv()
                total = total + zrecv[t, c, k].astype(F32)
        cvals[t, c, m] = total.astype(BF16)

    def correct(t, c):
        ls = pl.ds(c * width, width)
        chosen = dot(pick[...], cvals[t, c].reshape(MEMBERS * SHARE, width)).astype(BF16)
        for s in range(SIDE):
            rows = slice(s * INNER, (s + 1) * INNER)
            total = fine[rows, ls] + dot(bint[rows, :], chosen)
            total = total.reshape(SIDE, CELL, width)
            if t == 0:
                out[s, :, :, ls] = uext[s + 1, 1:1 + SIDE, :, ls] + total
                uext[s + 1, 1:1 + SIDE, :, ls] = total
            else:
                out[s, :, :, ls] = out[s, :, :, ls] + total

    def start_all(copies):
        for copy in copies:
            copy.start()

    def recv_all(copies):
        for copy in copies:
            copy.wait_recv()

    chunks = range(nch)
    loads[0].wait()
    for c in chunks:
        stencil(0, c)
    pl.semaphore_wait(barrier, len(partners))
    for t in range(SWEEPS):
        for c in chunks:
            if t:
                stencil(t, c)
            start_all(halo_copies(t, c))
        if t == 0:
            tables()
            loads[1].wait()
            expand_basis()
        for c in chunks:
            recv_all(halo_copies(t, c))
            finish_residual(t, c)
            restrict(t, c)
            start_all(gather_one(t, c))
        if t == 0:
            for copy in loads[2:]:
                copy.wait()
            expand_inverse()
        for c in chunks:
            fine_product(c)
        for c in chunks:
            recv_all(gather_one(t, c))
            coarse(t, c)
        for c in chunks:
            reduce_sums(t, c)
            start_all(gather_two(t, c))
        for c in chunks:
            recv_all(gather_two(t, c))
            correct(t, c)
    for t in range(SWEEPS):
        for c in chunks:
            for copy in (
                halo_copies(t, c) + gather_one(t, c) + core_copies(t, c)
                + y_copies(t, c) + z_copies(t, c)[1:] + gather_two(t, c)
            ):
                copy.wait_send()


def shards(nch, rhs, start, stiffness, sub_inverse, basis, coarse_inverse, offsets):
    def cells(field):
        flat = field.reshape(SIDE, SIDE, ROWS, LANES)
        return jnp.pad(flat, ((0, 0), (0, 0), (0, CELL - ROWS), (0, 0)))

    diag = (6.0 + stiffness).reshape(SIDE, SIDE, ROWS)
    diag = jnp.pad(diag, ((0, 0), (0, 0), (0, CELL - ROWS)))
    diag = jnp.broadcast_to(diag[..., None], (SIDE, SIDE, CELL, 128))
    width = LANES // nch
    lead = (SWEEPS, nch)
    vmem = pl.BlockSpec(memory_space=pltpu.VMEM)
    hbm = pl.BlockSpec(memory_space=pl.ANY)
    dma = pltpu.SemaphoreType.DMA
    out = pl.pallas_call(
        functools.partial(kernel, nch),
        name="schwarz",
        out_shape=jax.ShapeDtypeStruct((SIDE, SIDE, CELL, LANES), F32),
        in_specs=[pl.BlockSpec(memory_space=pltpu.SMEM), hbm, vmem, vmem, hbm, hbm, hbm],
        out_specs=vmem,
        scratch_shapes=[
            pltpu.VMEM((EXT, EXT, CELL, LANES), F32),
            pltpu.VMEM((SIDE, SIDE, CELL, LANES), F32),
            pltpu.VMEM((EXT, EXT, CELL, LANES), BF16),
            pltpu.VMEM((NLOC, LANES), BF16),
            pltpu.VMEM((SIDE, INNER, NLOC), BF16),
            pltpu.VMEM((SIDE * INNER, NLOC), BF16),
            pltpu.VMEM((NLOC, KMAX), BF16),
            pltpu.VMEM((SIDE * INNER, KMAX), BF16),
            pltpu.VMEM((KMAX, EXT * PADSLAB), BF16),
            pltpu.VMEM((2, 2 * NZ, SHARE, KGROUP), BF16),
            pltpu.VMEM((KGROUP, MEMBERS * KMAX), BF16),
            pltpu.VMEM((KMAX, KGROUP), BF16),
            pltpu.VMEM((SIDE * INNER, LANES), F32),
            pltpu.VMEM((nch, 2, NZ, SHARE, width), F32),
            pltpu.VMEM(lead + (4, 2, SIDE, CELL, width), BF16),
            pltpu.VMEM(lead + (4, 2, SIDE, CELL, width), BF16),
            pltpu.VMEM(lead + (4, 2, CELL, width), BF16),
            pltpu.VMEM(lead + (4, 2, CELL, width), BF16),
            pltpu.VMEM(lead + (MEMBERS, KMAX, width), BF16),
            pltpu.VMEM(lead + (2, NZ, SHARE, width), BF16),
            pltpu.VMEM(lead + (2, NZ, SHARE, width), BF16),
            pltpu.VMEM(lead + (NZ, SHARE, width), BF16),
            pltpu.VMEM(lead + (NZ, SHARE, width), BF16),
            pltpu.VMEM(lead + (NZ, SHARE, width), BF16),
            pltpu.VMEM(lead + (NZ, SHARE, width), BF16),
            pltpu.VMEM(lead + (MEMBERS, SHARE, width), BF16),
            dma((4 + SIDE,)),
            dma(lead + (8,)), dma(lead + (8,)),
            dma(lead + (8,)), dma(lead + (8,)),
            dma(lead + (2,)), dma(lead + (2,)),
            dma(lead + (8,)), dma(lead + (8,)),
            dma(lead + (8,)), dma(lead + (8,)),
            dma(lead + (8,)), dma(lead + (8,)),
        ],
        compiler_params=pltpu.CompilerParams(
            collective_id=0, has_side_effects=True, vmem_limit_bytes=56 * 1024 * 1024
        ),
    )(
        offsets[0],
        cells(start),
        cells(rhs),
        diag,
        sub_inverse[0],
        basis[0],
        coarse_inverse.reshape(2 * NZ, 2, SHARE, KGROUP),
    )
    return out[:, :, :ROWS, :].reshape(rhs.shape)


def solution(mesh):
    return jax.shard_map(
        functools.partial(shards, 1),
        mesh=mesh,
        in_specs=(
            P("sub", ("crow", "ccol"), None, None, None),
            P("sub", ("crow", "ccol"), None, None, None),
            P("sub", ("crow", "ccol"), None, None),
            P(("sub", "crow", "ccol"), None, None),
            P(("sub", "crow", "ccol"), None, None),
            P(None, ("crow", "ccol"), "sub"),
            P("sub", None),
        ),
        out_specs=P("sub", ("crow", "ccol"), None, None, None),
        check_vma=False,
    )
```

time: 571 us -> 113 us (0.20); the launches traced: 561 us -> 112 us
  blocking collectives: 378 us -> 0 us
  Pallas kernels: 0 us -> 102 us
  starting transfers between devices: 54.7 us -> 0 us
  waiting for transfers between devices: 53.7 us -> 0 us
  matrix products: 28.4 us -> 0 us
  other arithmetic: 18.3 us -> 0.02 us
  local copies, waits for them, and re-layouts: 27.4 us -> 10.6 us
    psum x2 -> x0, blocking collectives: 246 us -> none  [shards(): summed = lax.psum(partial_value, 'sub')]
    all_gather x4 -> x0, blocking collectives: 132 us -> none  [the longest x2 69.1 us: shards(): piece = lax.all_gather(amounts, ('crow', 'ccol'), axis=0, tiled=True)]
    pallas_call x0 -> x1, Pallas kernels: none -> 102 us  [shards(): pl.pallas_call(functools.partial(kernel, nch), name='schwarz', out_shape=...]
    ppermute x16 -> x0, starting transfers between devices: 54.7 us -> none  [the longest x8 32.3 us: extended_2(): lax.ppermute(lax.slice_in_dim(block, block.shape[dim] - width, None, axis...]
    ppermute x16 -> x0, waiting for transfers between devices: 53.7 us -> none  [the longest x8 27.6 us: extended_2(): lax.ppermute(lax.slice_in_dim(block, 0, width, axis=dim), axis, backward)]
    dot_general x8 -> x0, matrix products: 28.4 us -> none  [the longest x2 15.2 us: shards(): jnp.dot(local_inverse, flat_res, preferred_element_type=jnp.float32)]
    reshape x4, local copies, waits for them, and re-layouts: 13.1 us -> 2.66 us  [the longest x1 1.87 us: shards(): return out[:, :, :ROWS, :].reshape(rhs.shape)]
    add x3 -> x0, local copies, waits for them, and re-layouts: 7.76 us -> none  [the longest x2 5.72 us: shards(): fine_part + coarse_part]
  transfers between devices with their start and end apart: 16 -> 0, of which waited for: 14 -> 0; matrix products, arithmetic and copies ran while one was open for 1% -> 0% of each run, Pallas kernels for 0% -> 0%
where the time goes in v1:
time: 113 us; the launch traced here: 112 us
  Pallas kernels  102 us (90%)
  local copies, waits for them, and re-layouts  10.6 us (9%)
    pallas_call x1, Pallas kernels, shards(): pl.pallas_call(functools.partial(kernel, nch), name='schwarz', out_shape=...  102 us
    unnamed x6, local copies, waits for them, and re-layouts  2.77 us

profile of v1, /device:TPU:32, one launch (start us, length us, event | category | flops | bytes accessed | tf_op | source)
XLA Modules:
  0.0 112.2 jit_solution(9398784538004621436)
XLA Ops:
  0.0 1.7 %copy.11 = f32[6,6,3,10,256]{4,1,3,2,0:T(8,128)S(1)} copy(f32[6,6,3,10,256]{4,2,3,1,0:T(4,128)} %param.8) | data formatting | bytes 2211840 | tf_op args[1]
  1.7 0.3 copy.12
  2.1 0.0 copy-start
  2.1 1.1 pad.11.start_hbm
  3.2 0.7 copy-done
  3.9 0.4 copy.13
  4.2 0.3 copy.14
  4.6 0.0 copy-start.1
  4.6 1.1 pad.12.rhs
  5.7 0.0 copy-done.1
  5.7 0.1 reshape.18
  5.8 1.0 broadcast_in_dim.2.diag
  6.9 101.6 %schwarz.1 = f32[6,6,32,256]{3,2,1,0:T(8,128)} custom-call(s32[8]{0:T(128)} %bitcast.15, f32[6,6,32,256]{3,2,1,0:T(8,128)} %pad.11.start_hbm, f32[6,6,32,256]{3,2,1,0:T(8,128)} %pad.12.rhs, f32[6,6,32,128]{3,2,1,0:T(8,128)} %broadcast_in_dim.2.diag, bf16[1920,1920]{1,0:T(8,128)(2,1)} %bitcast.8, bf16[1920,128]{1,0:T(8,128)(2,1)} %bitcast.14, ...), custom_call_target="tpu_custom_call" | custom-call | tf_op jit(solution)/shard_map/schwarz/pallas_call | solution.py:477
  108.4 1.9 %copy.15 = f32[6,6,30,256]{3,1,2,0:T(8,128)S(1)} copy(f32[6,6,30,256]{3,2,1,0:T(8,128)} %bitcast.12) | data formatting | bytes 2211840 | tf_op jit(solution)/shard_map/slice | solution.py:530
  110.4 1.9 %copy.16 = f32[6,6,3,10,256]{4,2,3,1,0:T(4,128)} copy(f32[6,6,3,10,256]{4,1,3,2,0:T(8,128)S(1)} %bitcast.9) | data formatting | bytes 2211840 | tf_op jit(solution)/shard_map/reshape | solution.py:530
  (2 shorter events, 0.0 us)
Async XLA Ops:
  2.1 1.8 %copy-start = (f32[6,6,3,10,256]{4,2,3,1,0:T(4,128)S(1)}, f32[6,6,3,10,256]{4,2,3,1,0:T(4,128)}, u32[]{:S(2)}) copy-start(f32[6,6,3,10,256]{4,2,3,1,0:T(4,128)} %param.7) | copy-start | bytes 3317764
  4.6 1.1 copy-start.1

commit v2 on v1

--- a/solution.py
+++ b/solution.py
@@ -24,6 +24,8 @@
 SHARE = 64
 NZ = 8
 ZORDER = (4, 3, 5, 2, 6, 1, 7, 0)
+SPOT = (0, 2, 3, 4, 5, 1)
+GORDER = (5, 3, 7, 1, 4, 2, 6)
 F32 = jnp.float32
 BF16 = jnp.bfloat16
 
@@ -44,12 +46,16 @@
     nch,
     offs,
     start_hbm,
-    rhs,
-    diag,
+    rhs_hbm,
+    stiff,
     w_hbm,
     basis_hbm,
     c_hbm,
     out,
+    start_raw,
+    rhs_raw,
+    diag,
+    sol,
     uext,
     res,
     loc,
@@ -60,14 +66,14 @@
     bint,
     bt,
     cbuf,
+    coef,
     place,
     pick,
     fine,
     pb,
     hsend,
     hrecv,
-    csend_corner,
-    crecv_corner,
+    corners,
     pieces,
     cores,
     corer,
@@ -79,6 +85,8 @@
     load_sem,
     halo_s,
     halo_r,
+    corner_s,
+    corner_r,
     g1_s,
     g1_r,
     core_s,
@@ -107,10 +115,7 @@
 
     gp, gm = lax.rem(g + 1, 32), lax.rem(g + 31, 32)
     mp, mm = lax.rem(m + 1, MEMBERS), lax.rem(m + 7, MEMBERS)
-    halo_to = [
-        at(gp, m), at(gm, m), at(g, mp), at(g, mm),
-        at(gp, mp), at(gp, mm), at(gm, mp), at(gm, mm),
-    ]
+    halo_to = [at(gp, m), at(gm, m), at(g, mp), at(g, mm)]
     group_to = [at(g, lax.rem(m + j, MEMBERS)) for j in range(MEMBERS)]
     core_to = at(sub_of(ylo, z, 1 - core), m)
     y_to = at(sub_of(1 - ylo, z, core), m)
@@ -122,9 +127,8 @@
         pl.semaphore_signal(barrier, inc=1, device_id=device, device_id_type=MESH)
 
     loads = [
-        pltpu.make_async_copy(
-            start_hbm, uext.at[pl.ds(1, SIDE), pl.ds(1, SIDE)], load_sem.at[0]
-        ),
+        pltpu.make_async_copy(start_hbm, start_raw, load_sem.at[0]),
+        pltpu.make_async_copy(rhs_hbm, rhs_raw, load_sem.at[4 + SIDE]),
         pltpu.make_async_copy(basis_hbm, braw, load_sem.at[1]),
         pltpu.make_async_copy(c_hbm.at[:, 0], cbuf.at[0], load_sem.at[2]),
         pltpu.make_async_copy(c_hbm.at[:, 1], cbuf.at[1], load_sem.at[3]),
@@ -143,6 +147,7 @@
     for s in range(1, EXT - 1):
         uext[s, 0] = zero_row[0]
         uext[s, EXT - 1] = zero_row[0]
+        uext[s, 1:EXT - 1, 24:CELL, :] = jnp.zeros((SIDE, CELL - 24, LANES), F32)
 
     row = iota((CELL, 128), 0)
     layer = lax.rem(row, 10)
@@ -160,30 +165,50 @@
             device_id_type=MESH,
         )
 
-    def halo_copies(t, c):
-        out_copies = []
-        for d in range(4):
-            out_copies.append(
-                remote(
-                    hsend.at[t, c, d], hrecv.at[t, c, d],
-                    halo_s.at[t, c, d], halo_r.at[t, c, d], halo_to[d],
-                )
-            )
-        for d in range(4):
-            out_copies.append(
-                remote(
-                    csend_corner.at[t, c, d], crecv_corner.at[t, c, d],
-                    halo_s.at[t, c, 4 + d], halo_r.at[t, c, 4 + d], halo_to[4 + d],
-                )
-            )
-        return out_copies
+    def halo_copies(t, c, part, sides):
+        where = pl.ds(0, 2) if part == 0 else pl.ds(2, 4)
+        return [
+            remote(
+                hsend.at[t, c, d, :, where], hrecv.at[t, c, d, :, where],
+                halo_s.at[t, c, part, d], halo_r.at[t, c, part, d], halo_to[d],
+            )
+            for d in sides
+        ]
+
+    def corner_copies(t, c):
+        return [
+            remote(
+                hrecv.at[t, c, side, :, end], corners.at[t, c, d],
+                corner_s.at[t, c, d], corner_r.at[t, c, d], halo_to[to],
+            )
+            for d, side, end, to in ((0, 2, 1, 0), (1, 3, 1, 0), (2, 2, 0, 1), (3, 3, 0, 1))
+        ]
+
+    def unpack_inputs():
+        first = lax.rem(iota((CELL, 10), 0), 10) == iota((CELL, 10), 1)
+        comp = iota((CELL, 10), 0) // 10
+
+        def step(s, carry):
+            for q in range(SIDE):
+                k = stiff[s, q]
+                spread = jnp.where(comp == 0, k[0:1], jnp.where(comp == 1, k[1:2], k[2:3]))
+                column = jnp.sum(jnp.where(first, spread, 0.0), axis=1, keepdims=True)
+                diag[s, q] = jnp.broadcast_to(6.0 + column, (CELL, 128))
+                for lane in range(0, LANES, 128):
+                    ls = pl.ds(lane, 128)
+                    res[s, q, pl.ds(24, 8), ls] = jnp.zeros((8, 128), F32)
+                    for comp_id in range(3):
+                        rows = pl.ds(comp_id * 10, 10)
+                        uext[s + 1, q + 1, rows, ls] = start_raw[s, q, :, comp_id, ls]
+                        res[s, q, rows, ls] = rhs_raw[s, q, :, comp_id, ls]
+            return carry
+
+        lax.fori_loop(0, SIDE, step, 0)
 
     def lane_tiles(c):
         return [(c * width + i * 128, i * 128) for i in range(width // 128)]
 
     def stencil(t, c):
-        base = rhs if t == 0 else res
-
         def step(s, carry):
             for lane, _ in lane_tiles(c):
                 ls = pl.ds(lane, 128)
@@ -195,7 +220,7 @@
                     )
                     beside = beside + jnp.where(has_below, pltpu.roll(u, 1, 0), 0.0)
                     beside = beside + jnp.where(has_above, pltpu.roll(u, CELL - 1, 0), 0.0)
-                    res[s, q, :, ls] = base[s, q, :, ls] - (diag[s, q] * u - beside)
+                    res[s, q, :, ls] = res[s, q, :, ls] - (diag[s, q] * u - beside)
             return carry
 
         lax.fori_loop(0, SIDE, step, 0)
@@ -203,21 +228,18 @@
             ls, ds = pl.ds(lane, 128), pl.ds(dst, 128)
             for i in range(SIDE):
                 for d, (s, q) in enumerate(((SIDE - 1, i), (0, i), (i, SIDE - 1), (i, 0))):
-                    hsend[t, c, d, 0, i, :, ds] = uext[s + 1, q + 1, :, ls].astype(BF16)
-                    hsend[t, c, d, 1, i, :, ds] = res[s, q, :, ls].astype(BF16)
-            for d, (s, q) in enumerate(((5, 5), (5, 0), (0, 5), (0, 0))):
-                csend_corner[t, c, d, 0, :, ds] = uext[s + 1, q + 1, :, ls].astype(BF16)
-                csend_corner[t, c, d, 1, :, ds] = res[s, q, :, ls].astype(BF16)
+                    hsend[t, c, d, 0, SPOT[i], :, ds] = uext[s + 1, q + 1, :, ls].astype(BF16)
+                    hsend[t, c, d, 1, SPOT[i], :, ds] = res[s, q, :, ls].astype(BF16)
 
     def finish_residual(t, c):
         for lane, dst in lane_tiles(c):
             ls, ds = pl.ds(lane, 128), pl.ds(dst, 128)
 
             def got(d, field, i, ok):
-                return jnp.where(ok, hrecv[t, c, d, field, i, :, ds].astype(F32), 0.0)
+                return jnp.where(ok, hrecv[t, c, d, field, SPOT[i], :, ds].astype(F32), 0.0)
 
             def corner(d, field, ok):
-                return jnp.where(ok, crecv_corner[t, c, d, field, :, ds].astype(F32), 0.0)
+                return jnp.where(ok, corners[t, c, d, field, :, ds].astype(F32), 0.0)
 
             oks = (ok_sm, ok_sp, ok_qm, ok_qp)
             diag_ok = (
@@ -239,7 +261,7 @@
             for d in range(4):
                 for i in range(SIDE):
                     s, q = ((0, i), (5, i), (i, 0), (i, 5))[d]
-                    value = hrecv[t, c, d, 1, i, :, ds].astype(F32) + uext[s + 1, q + 1, :, ls]
+                    value = hrecv[t, c, d, 1, SPOT[i], :, ds].astype(F32) + uext[s + 1, q + 1, :, ls]
                     if i == 0:
                         value = value + cu[(0, 2, 0, 1)[d]]
                     if i == SIDE - 1:
@@ -250,9 +272,9 @@
             for d in range(4):
                 sd, qd = ((0, 2), (0, 3), (1, 2), (1, 3))[d]
                 si, qi = ((0, 0), (5, 0), (0, 5), (5, 5))[d]
-                value = crecv_corner[t, c, d, 1, :, ds].astype(F32)
-                value = value + hrecv[t, c, sd, 0, si, :, ds].astype(F32)
-                value = value + hrecv[t, c, qd, 0, qi, :, ds].astype(F32)
+                value = corners[t, c, d, 1, :, ds].astype(F32)
+                value = value + hrecv[t, c, sd, 0, SPOT[si], :, ds].astype(F32)
+                value = value + hrecv[t, c, qd, 0, SPOT[qi], :, ds].astype(F32)
                 value = jnp.where(diag_ok[d], value, 0.0).astype(BF16)
                 s, q = ((0, 0), (0, 7), (7, 0), (7, 7))[d]
                 loc[s, q, :, ls] = value
@@ -305,7 +327,7 @@
                 pieces.at[t, c, m], pieces.at[t, c, m],
                 g1_s.at[t, c, j], g1_r.at[t, c, j], group_to[j],
             )
-            for j in range(1, MEMBERS)
+            for j in GORDER
         ]
 
     def gather_two(t, c):
@@ -314,7 +336,7 @@
                 cvals.at[t, c, m], cvals.at[t, c, m],
                 g2_s.at[t, c, j], g2_r.at[t, c, j], group_to[j],
             )
-            for j in range(1, MEMBERS)
+            for j in GORDER
         ]
 
     def restrict(t, c):
@@ -363,39 +385,57 @@
             for k in range(NZ)
         ]
 
+    def block(t, c, own, half):
+        side = core if own else 1 - core
+        return cbuf[side, pl.ds(half * NZ, NZ)].reshape(NZ * SHARE, KGROUP)
+
     def coarse(t, c):
-        coef = dot(place[...], pieces[t, c].reshape(MEMBERS * KMAX, width)).astype(BF16)
+        coef[:, pl.ds(c * width, width)] = dot(
+            place[...], pieces[t, c].reshape(MEMBERS * KMAX, width)
+        ).astype(BF16)
         copies = core_copies(t, c)
-        for h, half in ((0, 1 - ylo), (1, ylo)):
-            rows = cbuf[1 - core, pl.ds(half * NZ, NZ)].reshape(NZ * SHARE, KGROUP)
-            cores[t, c, h] = dot(rows, coef).astype(BF16).reshape(NZ, SHARE, width)
-            copies[h].start()
-        for h, half in ((0, 1 - ylo), (1, ylo)):
-            rows = cbuf[core, pl.ds(half * NZ, NZ)].reshape(NZ * SHARE, KGROUP)
-            pb[c, h] = dot(rows, coef).reshape(NZ, SHARE, width)
+
+        def product(own, half):
+            return dot(block(t, c, own, half), coef[:, pl.ds(c * width, width)]).reshape(
+                NZ, SHARE, width
+            )
+
+        cores[t, c, 0] = product(False, 1 - ylo).astype(BF16)
+        copies[0].start()
+        pb[c, 0] = product(True, 1 - ylo)
+        cores[t, c, 1] = product(False, ylo).astype(BF16)
+        copies[1].start()
 
     def reduce_sums(t, c):
         copies, ys, zs = core_copies(t, c), y_copies(t, c), z_copies(t, c)
-        copies[0].wait_recv()
-        for k in ZORDER:
-            zz = lax.rem(z + k, NZ)
-            ysend[t, c, k] = (pb[c, 0, zz] + corer[t, c, 0, zz].astype(F32)).astype(BF16)
-            ys[k].start()
-        copies[1].wait_recv()
-        for k in ZORDER:
-            zz = lax.rem(z + k, NZ)
-            ys[k].wait_recv()
-            value = pb[c, 1, zz] + corer[t, c, 1, zz].astype(F32) + yrecv[t, c, k].astype(F32)
-            if k == 0:
-                total = value
-            else:
-                zsend[t, c, k] = value.astype(BF16)
-                zs[k].start()
-        for k in ZORDER[::-1]:
-            if k:
-                zs[k].wait_recv()
-                total = total + zrecv[t, c, k].astype(F32)
-        cvals[t, c, m] = total.astype(BF16)
+        with jax.named_scope("core0"):
+            copies[0].wait_recv()
+        with jax.named_scope("ysend"):
+            for k in ZORDER:
+                zz = lax.rem(z + k, NZ)
+                ysend[t, c, k] = (pb[c, 0, zz] + corer[t, c, 0, zz].astype(F32)).astype(BF16)
+                ys[k].start()
+            pb[c, 1] = dot(block(t, c, True, ylo), coef[:, pl.ds(c * width, width)]).reshape(
+                NZ, SHARE, width
+            )
+        with jax.named_scope("core1"):
+            copies[1].wait_recv()
+        with jax.named_scope("ywait"):
+            for k in ZORDER:
+                zz = lax.rem(z + k, NZ)
+                ys[k].wait_recv()
+                value = pb[c, 1, zz] + corer[t, c, 1, zz].astype(F32) + yrecv[t, c, k].astype(F32)
+                if k == 0:
+                    total = value
+                else:
+                    zsend[t, c, k] = value.astype(BF16)
+                    zs[k].start()
+        with jax.named_scope("zwait"):
+            for k in ZORDER[::-1]:
+                if k:
+                    zs[k].wait_recv()
+                    total = total + zrecv[t, c, k].astype(F32)
+            cvals[t, c, m] = total.astype(BF16)
 
     def correct(t, c):
         ls = pl.ds(c * width, width)
@@ -405,10 +445,16 @@
             total = fine[rows, ls] + dot(bint[rows, :], chosen)
             total = total.reshape(SIDE, CELL, width)
             if t == 0:
-                out[s, :, :, ls] = uext[s + 1, 1:1 + SIDE, :, ls] + total
+                sol[s, :, :, ls] = uext[s + 1, 1:1 + SIDE, :, ls] + total
                 uext[s + 1, 1:1 + SIDE, :, ls] = total
             else:
-                out[s, :, :, ls] = out[s, :, :, ls] + total
+                sol[s, :, :, ls] = sol[s, :, :, ls] + total
+                for q in range(SIDE):
+                    for lane, _ in lane_tiles(c):
+                        for comp_id in range(3):
+                            out[s, q, :, comp_id, pl.ds(lane, 128)] = sol[
+                                s, q, pl.ds(comp_id * 10, 10), pl.ds(lane, 128)
+                            ]
 
     def start_all(copies):
         for copy in copies:
@@ -418,57 +464,71 @@
         for copy in copies:
             copy.wait_recv()
 
+    def scoped(name, func, *args):
+        with jax.named_scope(name):
+            func(*args)
+
     chunks = range(nch)
-    loads[0].wait()
+    scoped("load0", loads[0].wait)
+    scoped("load0", loads[1].wait)
+    scoped("unpack", unpack_inputs)
     for c in chunks:
-        stencil(0, c)
-    pl.semaphore_wait(barrier, len(partners))
+        scoped("stencil", stencil, 0, c)
+    scoped("barrier", pl.semaphore_wait, barrier, len(partners))
     for t in range(SWEEPS):
         for c in chunks:
             if t:
-                stencil(t, c)
-            start_all(halo_copies(t, c))
+                scoped("stencil", stencil, t, c)
+            for part in range(2):
+                scoped("halo_send", start_all, halo_copies(t, c, part, (2, 3)))
+                scoped("halo_send", start_all, halo_copies(t, c, part, (0, 1)))
         if t == 0:
-            tables()
-            loads[1].wait()
-            expand_basis()
-        for c in chunks:
-            recv_all(halo_copies(t, c))
-            finish_residual(t, c)
-            restrict(t, c)
-            start_all(gather_one(t, c))
+            scoped("tables", tables)
+            scoped("load1", loads[2].wait)
+            scoped("basis", expand_basis)
+        for c in chunks:
+            scoped("end_wait", recv_all, halo_copies(t, c, 0, (2, 3)))
+            scoped("end_send", start_all, corner_copies(t, c))
         if t == 0:
-            for copy in loads[2:]:
-                copy.wait()
-            expand_inverse()
-        for c in chunks:
-            fine_product(c)
-        for c in chunks:
-            recv_all(gather_one(t, c))
-            coarse(t, c)
+            for copy in loads[3:]:
+                scoped("load2", copy.wait)
+            scoped("inverse", expand_inverse)
+        for c in chunks:
+            scoped("halo_s", recv_all, halo_copies(t, c, 0, (0, 1)) + halo_copies(t, c, 1, (0, 1)))
+            scoped("halo_q", recv_all, halo_copies(t, c, 1, (2, 3)))
+            scoped("corner", recv_all, corner_copies(t, c))
+            scoped("finish", finish_residual, t, c)
+            scoped("restrict", restrict, t, c)
+            scoped("g1_send", start_all, gather_one(t, c))
+        for c in chunks:
+            scoped("fine", fine_product, c)
+        for c in chunks:
+            scoped("g1_wait", recv_all, gather_one(t, c))
+            scoped("coarse", coarse, t, c)
         for c in chunks:
             reduce_sums(t, c)
-            start_all(gather_two(t, c))
-        for c in chunks:
-            recv_all(gather_two(t, c))
-            correct(t, c)
+            scoped("g2_send", start_all, gather_two(t, c))
+        for c in chunks:
+            scoped("g2_wait", recv_all, gather_two(t, c))
+            scoped("correct", correct, t, c)
     for t in range(SWEEPS):
         for c in chunks:
             for copy in (
-                halo_copies(t, c) + gather_one(t, c) + core_copies(t, c)
+                halo_copies(t, c, 0, range(4)) + halo_copies(t, c, 1, range(4))
+                + corner_copies(t, c)
+                + gather_one(t, c) + core_copies(t, c)
                 + y_copies(t, c) + z_copies(t, c)[1:] + gather_two(t, c)
             ):
                 copy.wait_send()
 
 
 def shards(nch, rhs, start, stiffness, sub_inverse, basis, coarse_inverse, offsets):
-    def cells(field):
-        flat = field.reshape(SIDE, SIDE, ROWS, LANES)
-        return jnp.pad(flat, ((0, 0), (0, 0), (0, CELL - ROWS), (0, 0)))
-
-    diag = (6.0 + stiffness).reshape(SIDE, SIDE, ROWS)
-    diag = jnp.pad(diag, ((0, 0), (0, 0), (0, CELL - ROWS)))
-    diag = jnp.broadcast_to(diag[..., None], (SIDE, SIDE, CELL, 128))
+    def held(array):
+        return pltpu.with_memory_space_constraint(array, pltpu.HBM)
+
+    def turned(field):
+        return jnp.transpose(field, (0, 1, 3, 2, 4))
+
     width = LANES // nch
     lead = (SWEEPS, nch)
     vmem = pl.BlockSpec(memory_space=pltpu.VMEM)
@@ -477,10 +537,14 @@
     out = pl.pallas_call(
         functools.partial(kernel, nch),
         name="schwarz",
-        out_shape=jax.ShapeDtypeStruct((SIDE, SIDE, CELL, LANES), F32),
-        in_specs=[pl.BlockSpec(memory_space=pltpu.SMEM), hbm, vmem, vmem, hbm, hbm, hbm],
+        out_shape=jax.ShapeDtypeStruct((SIDE, SIDE, 10, 3, LANES), F32),
+        in_specs=[pl.BlockSpec(memory_space=pltpu.SMEM), hbm, hbm, vmem, hbm, hbm, hbm],
         out_specs=vmem,
         scratch_shapes=[
+            pltpu.VMEM((SIDE, SIDE, 10, 3, LANES), F32),
+            pltpu.VMEM((SIDE, SIDE, 10, 3, LANES), F32),
+            pltpu.VMEM((SIDE, SIDE, CELL, 128), F32),
+            pltpu.VMEM((SIDE, SIDE, CELL, LANES), F32),
             pltpu.VMEM((EXT, EXT, CELL, LANES), F32),
             pltpu.VMEM((SIDE, SIDE, CELL, LANES), F32),
             pltpu.VMEM((EXT, EXT, CELL, LANES), BF16),
@@ -491,13 +555,13 @@
             pltpu.VMEM((SIDE * INNER, KMAX), BF16),
             pltpu.VMEM((KMAX, EXT * PADSLAB), BF16),
             pltpu.VMEM((2, 2 * NZ, SHARE, KGROUP), BF16),
+            pltpu.VMEM((KGROUP, LANES), BF16),
             pltpu.VMEM((KGROUP, MEMBERS * KMAX), BF16),
             pltpu.VMEM((KMAX, KGROUP), BF16),
             pltpu.VMEM((SIDE * INNER, LANES), F32),
             pltpu.VMEM((nch, 2, NZ, SHARE, width), F32),
             pltpu.VMEM(lead + (4, 2, SIDE, CELL, width), BF16),
             pltpu.VMEM(lead + (4, 2, SIDE, CELL, width), BF16),
-            pltpu.VMEM(lead + (4, 2, CELL, width), BF16),
             pltpu.VMEM(lead + (4, 2, CELL, width), BF16),
             pltpu.VMEM(lead + (MEMBERS, KMAX, width), BF16),
             pltpu.VMEM(lead + (2, NZ, SHARE, width), BF16),
@@ -507,8 +571,9 @@
             pltpu.VMEM(lead + (NZ, SHARE, width), BF16),
             pltpu.VMEM(lead + (NZ, SHARE, width), BF16),
             pltpu.VMEM(lead + (MEMBERS, SHARE, width), BF16),
-            dma((4 + SIDE,)),
-            dma(lead + (8,)), dma(lead + (8,)),
+            dma((5 + SIDE,)),
+            dma(lead + (2, 4)), dma(lead + (2, 4)),
+            dma(lead + (4,)), dma(lead + (4,)),
             dma(lead + (8,)), dma(lead + (8,)),
             dma(lead + (2,)), dma(lead + (2,)),
             dma(lead + (8,)), dma(lead + (8,)),
@@ -516,18 +581,18 @@
             dma(lead + (8,)), dma(lead + (8,)),
         ],
         compiler_params=pltpu.CompilerParams(
-            collective_id=0, has_side_effects=True, vmem_limit_bytes=56 * 1024 * 1024
+            collective_id=0, has_side_effects=True, vmem_limit_bytes=44 * 1024 * 1024
         ),
     )(
-        offsets[0],
-        cells(start),
-        cells(rhs),
-        diag,
-        sub_inverse[0],
-        basis[0],
-        coarse_inverse.reshape(2 * NZ, 2, SHARE, KGROUP),
+        held(offsets[0]),
+        held(turned(start)),
+        held(turned(rhs)),
+        held(stiffness),
+        held(sub_inverse[0]),
+        held(basis[0]),
+        held(coarse_inverse.reshape(2 * NZ, 2, SHARE, KGROUP)),
     )
-    return out[:, :, :ROWS, :].reshape(rhs.shape)
+    return turned(out)
 
 
 def solution(mesh):

time: 113 us -> 95.8 us (0.85)
  local copies, waits for them, and re-layouts: 10.6 us -> 1.11 us
  Pallas kernels: 102 us -> 94.6 us
    pallas_call x1, Pallas kernels: 102 us -> 94.6 us  [shards(): pl.pallas_call(functools.partial(kernel, nch), name='schwarz', out_shape=...]
    reshape x4 -> x0, local copies, waits for them, and re-layouts: 2.66 us -> none  [the longest x1 1.87 us: shards(): return out[:, :, :ROWS, :].reshape(rhs.shape)]
    pad x3 -> x0, local copies, waits for them, and re-layouts: 2.21 us -> none  [the longest x2 2.21 us: cells(): return jnp.pad(flat, ((0, 0), (0, 0), (0, CELL - ROWS), (0, 0)))]
    slice x1 -> x0, local copies, waits for them, and re-layouts: 1.93 us -> none  [shards(): return out[:, :, :ROWS, :].reshape(rhs.shape)]
    unnamed x6 -> x1, local copies, waits for them, and re-layouts: 2.77 us -> 1.11 us
where the time goes in v2:
time: 95.8 us; the launch traced here: 95.7 us
  Pallas kernels  94.6 us (99%)
  local copies, waits for them, and re-layouts  1.11 us (1%)
    pallas_call x1, Pallas kernels, shards(): pl.pallas_call(functools.partial(kernel, nch), name='schwarz', out_shape=...  94.6 us

profile of v2, /device:TPU:32, one launch (start us, length us, event | category | flops | bytes accessed | tf_op | source)
XLA Modules:
  0.0 95.7 jit_solution(10557440607639829626)
XLA Ops:
  0.0 94.6 %schwarz.1 = f32[6,6,10,3,256]{4,3,2,1,0:T(4,128)S(1)} custom-call(s32[8]{0:T(128)} %bitcast.13, f32[6,6,10,3,256]{4,3,2,1,0:T(4,128)} %bitcast.10, f32[6,6,10,3,256]{4,3,2,1,0:T(4,128)} %bitcast.11, f32[6,6,3,10]{3,2,1,0:T(4,128)} %stiff.1, bf16[1920,1920]{1,0:T(8,128)(2,1)} %bitcast.8, bf16[1920,128]{1,0:T(8,128)(2,1)} %bitcast.12, ...), custom_call_target="tpu_custom_call" | custom-call | tf_op jit(solution)/shard_map/schwarz/pallas_call | solution.py:537
  94.6 1.1 %copy.9 = f32[6,6,3,10,256]{4,2,3,1,0:T(4,128)} copy(f32[6,6,3,10,256]{4,2,3,1,0:T(4,128)S(1)} %bitcast.7) | data formatting | bytes 2211840

commit v3 on v2

--- a/solution.py
+++ b/solution.py
@@ -406,36 +406,38 @@
         cores[t, c, 1] = product(False, ylo).astype(BF16)
         copies[1].start()
 
-    def reduce_sums(t, c):
+    def reduce_core(t, c):
+        copies, ys = core_copies(t, c), y_copies(t, c)
+        copies[0].wait_recv()
+        for k in ZORDER:
+            zz = lax.rem(z + k, NZ)
+            ysend[t, c, k] = (pb[c, 0, zz] + corer[t, c, 0, zz].astype(F32)).astype(BF16)
+            ys[k].start()
+        pb[c, 1] = dot(block(t, c, True, ylo), coef[:, pl.ds(c * width, width)]).reshape(
+            NZ, SHARE, width
+        )
+
+    def reduce_y(t, c):
         copies, ys, zs = core_copies(t, c), y_copies(t, c), z_copies(t, c)
-        with jax.named_scope("core0"):
-            copies[0].wait_recv()
-        with jax.named_scope("ysend"):
-            for k in ZORDER:
-                zz = lax.rem(z + k, NZ)
-                ysend[t, c, k] = (pb[c, 0, zz] + corer[t, c, 0, zz].astype(F32)).astype(BF16)
-                ys[k].start()
-            pb[c, 1] = dot(block(t, c, True, ylo), coef[:, pl.ds(c * width, width)]).reshape(
-                NZ, SHARE, width
-            )
-        with jax.named_scope("core1"):
-            copies[1].wait_recv()
-        with jax.named_scope("ywait"):
-            for k in ZORDER:
-                zz = lax.rem(z + k, NZ)
-                ys[k].wait_recv()
-                value = pb[c, 1, zz] + corer[t, c, 1, zz].astype(F32) + yrecv[t, c, k].astype(F32)
-                if k == 0:
-                    total = value
-                else:
-                    zsend[t, c, k] = value.astype(BF16)
-                    zs[k].start()
-        with jax.named_scope("zwait"):
-            for k in ZORDER[::-1]:
-                if k:
-                    zs[k].wait_recv()
-                    total = total + zrecv[t, c, k].astype(F32)
-            cvals[t, c, m] = total.astype(BF16)
+        copies[1].wait_recv()
+        for k in ZORDER:
+            zz = lax.rem(z + k, NZ)
+            ys[k].wait_recv()
+            value = pb[c, 1, zz] + corer[t, c, 1, zz].astype(F32) + yrecv[t, c, k].astype(F32)
+            if k == 0:
+                pb[c, 0, 0] = value
+            else:
+                zsend[t, c, k] = value.astype(BF16)
+                zs[k].start()
+
+    def reduce_z(t, c):
+        zs = z_copies(t, c)
+        total = pb[c, 0, 0]
+        for k in ZORDER[::-1]:
+            if k:
+                zs[k].wait_recv()
+                total = total + zrecv[t, c, k].astype(F32)
+        cvals[t, c, m] = total.astype(BF16)
 
     def correct(t, c):
         ls = pl.ds(c * width, width)
@@ -475,42 +477,57 @@
     for c in chunks:
         scoped("stencil", stencil, 0, c)
     scoped("barrier", pl.semaphore_wait, barrier, len(partners))
+    for c in chunks:
+        for part in range(2):
+            scoped("halo_send", start_all, halo_copies(0, c, part, (2, 3, 0, 1)))
     for t in range(SWEEPS):
-        for c in chunks:
-            if t:
-                scoped("stencil", stencil, t, c)
-            for part in range(2):
-                scoped("halo_send", start_all, halo_copies(t, c, part, (2, 3)))
-                scoped("halo_send", start_all, halo_copies(t, c, part, (0, 1)))
         if t == 0:
             scoped("tables", tables)
             scoped("load1", loads[2].wait)
             scoped("basis", expand_basis)
-        for c in chunks:
+        def residual_part(c):
             scoped("end_wait", recv_all, halo_copies(t, c, 0, (2, 3)))
             scoped("end_send", start_all, corner_copies(t, c))
-        if t == 0:
-            for copy in loads[3:]:
-                scoped("load2", copy.wait)
-            scoped("inverse", expand_inverse)
-        for c in chunks:
-            scoped("halo_s", recv_all, halo_copies(t, c, 0, (0, 1)) + halo_copies(t, c, 1, (0, 1)))
+
+        def restrict_part(c):
+            for part in range(2):
+                scoped("halo_s", recv_all, halo_copies(t, c, part, (0, 1)))
             scoped("halo_q", recv_all, halo_copies(t, c, 1, (2, 3)))
             scoped("corner", recv_all, corner_copies(t, c))
             scoped("finish", finish_residual, t, c)
             scoped("restrict", restrict, t, c)
             scoped("g1_send", start_all, gather_one(t, c))
-        for c in chunks:
-            scoped("fine", fine_product, c)
-        for c in chunks:
+
+        def coarse_part(c):
             scoped("g1_wait", recv_all, gather_one(t, c))
             scoped("coarse", coarse, t, c)
+
+        residual_part(0)
+        if t == 0:
+            for copy in loads[3:]:
+                scoped("load2", copy.wait)
+            scoped("inverse", expand_inverse)
+        restrict_part(0)
+        residual_part(1)
+        restrict_part(1)
+        scoped("fine", fine_product, 0)
+        coarse_part(0)
+        scoped("core", reduce_core, t, 0)
+        coarse_part(1)
+        scoped("core", reduce_core, t, 1)
+        scoped("y0", reduce_y, t, 0)
+        scoped("fine", fine_product, 1)
+        scoped("y1", reduce_y, t, 1)
         for c in chunks:
-            reduce_sums(t, c)
+            scoped("zwait", reduce_z, t, c)
             scoped("g2_send", start_all, gather_two(t, c))
         for c in chunks:
             scoped("g2_wait", recv_all, gather_two(t, c))
             scoped("correct", correct, t, c)
+            if t == 0:
+                scoped("stencil", stencil, 1, c)
+                for part in range(2):
+                    scoped("halo_send", start_all, halo_copies(1, c, part, (2, 3, 0, 1)))
     for t in range(SWEEPS):
         for c in chunks:
             for copy in (
@@ -597,7 +614,7 @@
 
 def solution(mesh):
     return jax.shard_map(
-        functools.partial(shards, 1),
+        functools.partial(shards, 2),
         mesh=mesh,
         in_specs=(
             P("sub", ("crow", "ccol"), None, None, None),

time: 95.8 us -> 92.9 us (0.970)
  Pallas kernels: 94.6 us -> 91.6 us
    pallas_call x1, Pallas kernels: 94.6 us -> 91.6 us  [shards(): pl.pallas_call(functools.partial(kernel, nch), name='schwarz', out_shape=...]
where the time goes in v3:
time: 92.9 us; the launch traced here: 92.7 us
  Pallas kernels  91.6 us (99%)
  local copies, waits for them, and re-layouts  1.11 us (1%)
    pallas_call x1, Pallas kernels, shards(): pl.pallas_call(functools.partial(kernel, nch), name='schwarz', out_shape=...  91.6 us

profile of v3, /device:TPU:32, one launch (start us, length us, event | category | flops | bytes accessed | tf_op | source)
XLA Modules:
  0.0 92.7 jit_solution(14128404724267278629)
XLA Ops:
  0.0 91.6 %schwarz.1 = f32[6,6,10,3,256]{4,3,2,1,0:T(4,128)S(1)} custom-call(s32[8]{0:T(128)} %bitcast.13, f32[6,6,10,3,256]{4,3,2,1,0:T(4,128)} %bitcast.10, f32[6,6,10,3,256]{4,3,2,1,0:T(4,128)} %bitcast.11, f32[6,6,3,10]{3,2,1,0:T(4,128)} %stiff.1, bf16[1920,1920]{1,0:T(8,128)(2,1)} %bitcast.8, bf16[1920,128]{1,0:T(8,128)(2,1)} %bitcast.12, ...), custom_call_target="tpu_custom_call" | custom-call | tf_op jit(solution)/shard_map/schwarz/pallas_call | solution.py:554
  91.6 1.1 %copy.9 = f32[6,6,3,10,256]{4,2,3,1,0:T(4,128)} copy(f32[6,6,3,10,256]{4,2,3,1,0:T(4,128)S(1)} %bitcast.7) | data formatting | bytes 2211840

commit v4 on v3

--- a/solution.py
+++ b/solution.py
@@ -503,12 +503,12 @@
             scoped("coarse", coarse, t, c)
 
         residual_part(0)
+        restrict_part(0)
+        residual_part(1)
         if t == 0:
             for copy in loads[3:]:
                 scoped("load2", copy.wait)
             scoped("inverse", expand_inverse)
-        restrict_part(0)
-        residual_part(1)
         restrict_part(1)
         scoped("fine", fine_product, 0)
         coarse_part(0)

time: 92.9 us -> 90.5 us (0.974)
  Pallas kernels: 91.6 us -> 89.2 us
    pallas_call x1, Pallas kernels: 91.6 us -> 89.2 us  [shards(): pl.pallas_call(functools.partial(kernel, nch), name='schwarz', out_shape=...]
where the time goes in v4:
time: 90.5 us; the launch traced here: 90.3 us
  Pallas kernels  89.2 us (99%)
  local copies, waits for them, and re-layouts  1.11 us (1%)
    pallas_call x1, Pallas kernels, shards(): pl.pallas_call(functools.partial(kernel, nch), name='schwarz', out_shape=...  89.2 us

profile of v4, /device:TPU:32, one launch (start us, length us, event | category | flops | bytes accessed | tf_op | source)
XLA Modules:
  0.0 90.3 jit_solution(10054105446543092422)
XLA Ops:
  0.0 89.2 %schwarz.1 = f32[6,6,10,3,256]{4,3,2,1,0:T(4,128)S(1)} custom-call(s32[8]{0:T(128)} %bitcast.13, f32[6,6,10,3,256]{4,3,2,1,0:T(4,128)} %bitcast.10, f32[6,6,10,3,256]{4,3,2,1,0:T(4,128)} %bitcast.11, f32[6,6,3,10]{3,2,1,0:T(4,128)} %stiff.1, bf16[1920,1920]{1,0:T(8,128)(2,1)} %bitcast.8, bf16[1920,128]{1,0:T(8,128)(2,1)} %bitcast.12, ...), custom_call_target="tpu_custom_call" | custom-call | tf_op jit(solution)/shard_map/schwarz/pallas_call | solution.py:554
  89.2 1.1 %copy.9 = f32[6,6,3,10,256]{4,2,3,1,0:T(4,128)} copy(f32[6,6,3,10,256]{4,2,3,1,0:T(4,128)S(1)} %bitcast.7) | data formatting | bytes 2211840
